TPU v7x, 512 devices: a whole 4x8x8 slice. The times are simulated.
512 devices in a mesh: gx: 16 (over z, x_lo), gy: 8 (over y), gz: 4 (over x_hi, core).
Axes of the slice: x: 4 (x_hi: 2, x_lo: 2; x = x_hi * 2 + x_lo), y: 8, z: 8, core: 2. Of those that a mesh axis runs over, the one named last changes fastest.
Arguments:
- block_input: bfloat16 [64, 64, 4096], P('gx', 'gy', 'gz'), may hold values from -6 to 6
- pre_act: bfloat16 [64, 64, 4096], P('gx', 'gy', 'gz'), may hold values from -6 to 6
- skip_grad: bfloat16 [64, 64, 4096], P('gx', 'gy', 'gz'), may hold values from -6 to 6
- pool_grad: bfloat16 [32, 32, 2048], P('gx', 'gy', 'gz'), may hold values from -6 to 6
- conv1_weight: bfloat16 [64, 1728], P('gx'), may hold values from -0.15625 to 0.15625
- conv2_weight: bfloat16 [64, 1728], P('gx'), may hold values from -0.15625 to 0.15625
Outputs:
- input_grad: bfloat16 [64, 64, 4096], P('gx', 'gy', 'gz')
- conv1_grad: float32 [64, 1728], P('gx')
- conv2_grad: float32 [64, 1728], P('gx')
All inputs are finite; a program needn't handle non-finite values.
Results may differ from a plain program's by a relative error of at most 0.0053.
Values may be sent and summed in bfloat16 or wider, within the bound.
No kernel may reach another device: no remote copies, remote signals or barrier semaphores. Data moves between devices by JAX's collectives and lax.ppermute only.
A program may use at most 64 MiB of HBM per device.

v0:
```python
import math
import jax
import jax.numpy as jnp
from jax import lax
from jax.sharding import PartitionSpec as P


def padded_2(block, sides, width):
    for axis, dim in sides:
        count = lax.axis_size(axis)
        forward = [(i, i + 1) for i in range(count - 1)]
        forward.append((count - 1, 0))
        backward = [(target, source) for source, target in forward]
        low = lax.ppermute(
            lax.slice_in_dim(block, block.shape[dim] - width, None, axis=dim), axis, forward
        )
        high = lax.ppermute(lax.slice_in_dim(block, 0, width, axis=dim), axis, backward)
        block = jnp.concatenate([low, block, high], axis=dim)
    return block


def offset_of(k):
    return (k // 9 - 1, k // 3 % 3 - 1, k % 3 - 1)


def silu_slope(v):
    g = jax.nn.sigmoid(v)
    return g * (1.0 + v * (1.0 - g))


def window(padded, start, shape):
    lower = (start[0], start[1], start[2], 0)
    upper = (start[0] + shape[0], start[1] + shape[1], start[2] + shape[2], padded.shape[3])
    return lax.slice(padded, lower, upper).reshape(-1, padded.shape[3])


def transpose_conv(weight, padded, margin, shape):
    chans = weight.shape[0]
    total = None
    for k in range(27):
        d = offset_of(k)
        behind = window(padded, (margin - d[0], margin - d[1], margin - d[2]), shape)
        block = weight[:, k * chans : (k + 1) * chans]
        term = lax.dot_general(
            behind, block, (((1,), (0,)), ((), ())), preferred_element_type=jnp.float32
        )
        total = term if total is None else total + term
    return total


def weight_grad(left_flat, padded, margin, shape):
    pieces = []
    for k in range(27):
        d = offset_of(k)
        ahead = window(padded, (margin + d[0], margin + d[1], margin + d[2]), shape)
        pieces.append(
            lax.dot_general(
                left_flat, ahead, (((0,), (0,)), ((), ())), preferred_element_type=jnp.float32
            )
        )
    return jnp.concatenate(pieces, axis=1)


def body(block_input, pre_act, skip_grad, pool_grad, conv1_weight, conv2_weight):
    chans = conv1_weight.shape[1] // 27
    size_x, size_y, merged = block_input.shape
    size_z = merged // chans
    inner = (size_x, size_y, size_z)
    four_shape = (size_x, size_y, size_z, chans)
    weight_one, weight_two = (
        lax.all_gather(conv1_weight, "gx", axis=0, tiled=True),
        lax.all_gather(conv2_weight, "gx", axis=0, tiled=True),
    )
    pool_four = pool_grad.reshape(size_x // 2, size_y // 2, size_z // 2, chans).astype(jnp.float32)
    upsampled = jnp.repeat(jnp.repeat(jnp.repeat(pool_four, 2, axis=0), 2, axis=1), 2, axis=2)
    out_grad = (skip_grad.reshape(four_shape).astype(jnp.float32) + 0.125 * upsampled).astype(
        jnp.bfloat16
    )
    out_flat = out_grad.reshape(-1, chans)
    input_four = block_input.reshape(four_shape)
    pre_four = pre_act.reshape(four_shape)
    stacked = jnp.concatenate([input_four, pre_four, out_grad], axis=3)
    padded = padded_2(stacked, (("gx", 0), ("gy", 1), ("gz", 2)), 1)
    input_pad = padded[..., :chans]
    act_pad = jax.nn.silu(padded[..., chans : 2 * chans].astype(jnp.float32)).astype(jnp.bfloat16)
    grad_pad = padded[..., 2 * chans :]
    grads_two = weight_grad(out_flat, act_pad, 1, inner)
    act_grad = transpose_conv(weight_two, grad_pad, 1, inner)
    slope = silu_slope(pre_four.astype(jnp.float32)).reshape(-1, chans)
    pre_grad = (act_grad * slope).astype(jnp.bfloat16).reshape(four_shape)
    pre_pad = padded_2(pre_grad, (("gx", 0), ("gy", 1), ("gz", 2)), 1)
    pre_flat = pre_grad.reshape(-1, chans)
    grads_one = weight_grad(pre_flat, input_pad, 1, inner)
    total = out_grad.astype(jnp.float32).reshape(-1, chans) + transpose_conv(
        weight_one, pre_pad, 1, inner
    )
    input_grad = total.reshape(size_x, size_y, merged).astype(jnp.bfloat16)
    cells_all = (
        inner[0]
        * inner[1]
        * inner[2]
        * lax.axis_size("gx")
        * lax.axis_size("gy")
        * lax.axis_size("gz")
    )
    scale_all = 1.0 / math.sqrt(cells_all)
    grads_one = grads_one * scale_all
    grads_two = grads_two * scale_all
    owned = chans // lax.axis_size("gx")
    summed_one, summed_two = lax.psum((grads_one, grads_two), ("gx", "gy", "gz"))
    first = lax.axis_index("gx") * owned
    conv1_grad = lax.dynamic_slice_in_dim(summed_one, first, owned, 0)
    conv2_grad = lax.dynamic_slice_in_dim(summed_two, first, owned, 0)
    return (input_grad, conv1_grad, conv2_grad)


def solution(mesh):
    in_specs = (
        P("gx", "gy", "gz"),
        P("gx", "gy", "gz"),
        P("gx", "gy", "gz"),
        P("gx", "gy", "gz"),
        P("gx", None),
        P("gx", None),
    )
    out_specs = (P("gx", "gy", "gz"), P("gx", None), P("gx", None))
    return jax.shard_map(body, mesh=mesh, in_specs=in_specs, out_specs=out_specs, check_vma=False)
```

profile of v0, /device:TPU:1, one launch (start us, length us, event | category | flops | bytes accessed | tf_op | source)
XLA Modules:
  0.0 442.2 jit_solution(9441771854849640452)
XLA Ops:
  7.2 1.0 reshape.404
  8.2 0.7 convert_multiply_fusion.1
  9.0 1.0 reshape.322
  10.0 1.0 reshape.321
  11.3 12.4 %collective-permute-start.1 = (bf16[1,8,16,192]{3,2,1,0:T(8,128)(2,1)S(1)}, bf16[1,8,16,192]{3,2,1,0:T(8,128)(2,1)S(1)}, u32[]{:S(2)}, u32[]{:S(2)}) collective-permute-start(bf16[1,8,16,192]{3,2,1,0:T(8,128)(2,1)S(1)} %get-tuple-element.68), channel_id=1, source_target_pairs={{32,0},{64,32},{96,64},{128,96},{160,128},{192,160},{224,192},{256... | collective-permute-start | bytes 147464 | tf_op jit(solution)/shard_map/ppermute | solution.py:17
  23.7 1.9 collective-permute-start
  26.1 27.4 %all-gather = bf16[16,4,1728]{2,1,0:T(4,128)(2,1)S(1)} all-gather(bf16[1,4,1728]{2,1,0:T(4,128)(2,1)S(1)} %bitcast.417), channel_id=1, replica_groups=mesh['gx'=16,'gy'=8,'gz'=4] {'gx'}, dimensions={0}, use_global_device_ids=true | all-gather | bytes 235008 | tf_op jit(solution)/shard_map/all_gather | solution.py:72
  53.9 0.9 fusion.86
  54.9 24.1 %all-gather.1 = bf16[16,4,1728]{2,1,0:T(4,128)(2,1)S(1)} all-gather(bf16[1,4,1728]{2,1,0:T(4,128)(2,1)S(1)} %bitcast.418), channel_id=1, replica_groups=mesh['gx'=16,'gy'=8,'gz'=4] {'gx'}, dimensions={0}, use_global_device_ids=true | all-gather | bytes 235008 | tf_op jit(solution)/shard_map/all_gather | solution.py:71
  79.3 0.8 copy.24
  80.2 5.1 %collective-permute-start.3 = (bf16[6,1,16,192]{3,2,1,0:T(8,128)(2,1)S(1)}, bf16[6,1,16,192]{3,2,1,0:T(8,128)(2,1)S(1)}, u32[]{:S(2)}, u32[]{:S(2)}) collective-permute-start(bf16[6,1,16,192]{3,2,1,0:T(8,128)(2,1)S(1)} %get-tuple-element.48), channel_id=1, source_target_pairs={{4,0},{8,4},{12,8},{16,12},{20,16},{24,20},{28,24},{0,28},{5,1},{9... | collective-permute-start | bytes 110600 | tf_op jit(solution)/shard_map/ppermute | solution.py:17
  85.3 1.9 collective-permute-start.2
  87.3 0.9 pad_maximum_fusion.10
  88.2 3.5 collective-permute-done.2
  91.9 18.2 %collective-permute-start.4 = (bf16[6,10,1,192]{3,2,1,0:T(2,128)(2,1)S(1)}, bf16[6,10,1,192]{3,2,1,0:T(2,128)(2,1)S(1)}, u32[]{:S(2)}, u32[]{:S(2)}) collective-permute-start(bf16[6,10,1,192]{3,2,1,0:T(2,128)(2,1)S(1)} %get-tuple-element.43), channel_id=1, source_target_pairs={{1,0},{2,1},{3,2},{0,3},{5,4},{6,5},{7,6},{4,7},{9,8},{10,9},{11,1... | collective-permute-start | bytes 69128 | tf_op jit(solution)/shard_map/ppermute | solution.py:17
  110.1 4.3 collective-permute-start.5
  115.2 0.5 collective-permute-done.5
  115.7 0.5 fusion.13
  116.2 0.8 convolution_bitcast_fusion.26
  117.0 0.8 convolution_bitcast_fusion.25
  117.8 0.8 convolution_bitcast_fusion.24
  118.7 0.8 convolution_bitcast_fusion.23
  119.5 0.8 convolution_bitcast_fusion.22
  120.3 0.8 convolution_bitcast_fusion.21
  121.1 0.8 convolution_bitcast_fusion.20
  121.9 0.8 convolution_bitcast_fusion.19
  122.7 0.8 convolution_bitcast_fusion.18
  123.5 0.8 convolution_bitcast_fusion.17
  124.3 0.8 convolution_bitcast_fusion.16
  125.1 0.8 convolution_bitcast_fusion.15
  125.9 0.8 convolution_bitcast_fusion.14
  126.7 0.8 convolution_bitcast_fusion.13
  127.5 0.8 convolution_bitcast_fusion.12
  128.3 0.8 convolution_bitcast_fusion.11
  129.1 0.8 convolution_bitcast_fusion.10
  130.0 0.8 convolution_bitcast_fusion.9
  130.8 0.8 convolution_bitcast_fusion.8
  131.6 0.8 convolution_bitcast_fusion.7
  132.4 0.8 convolution_bitcast_fusion.6
  133.2 0.8 convolution_bitcast_fusion.5
  134.0 0.8 convolution_bitcast_fusion.4
  134.8 0.8 convolution_bitcast_fusion.3
  135.6 0.8 convolution_bitcast_fusion.2
  136.4 0.8 convolution_bitcast_fusion.1
  137.2 0.8 convolution_bitcast_fusion
  138.0 1.4 pad_maximum_fusion
  140.3 1.3 fusion.103
  147.3 0.7 copy.28
  148.1 2.9 collective-permute-start.7
  151.0 0.7 copy.26
  151.7 2.3 collective-permute-start.6
  154.7 1.1 fusion.116
  159.8 0.8 broadcast_multiply_fusion.1
  161.1 0.8 broadcast_multiply_fusion
  162.4 2.1 collective-permute-start.9
  164.5 3.4 collective-permute-start.8
  167.9 2.4 collective-permute-done.8
  170.3 5.3 %collective-permute-start.10 = (bf16[6,10,1,64]{3,2,1,0:T(2,128)(2,1)S(1)}, bf16[6,10,1,64]{3,2,1,0:T(2,128)(2,1)S(1)}, u32[]{:S(2)}, u32[]{:S(2)}) collective-permute-start(bf16[6,10,1,64]{3,2,1,0:T(2,128)(2,1)S(1)} %get-tuple-element.89), channel_id=1, source_target_pairs={{1,0},{2,1},{3,2},{0,3},{5,4},{6,5},{7,6},{4,7},{9,8},{10,9},{11,1... | collective-permute-start | bytes 23048 | tf_op jit(solution)/shard_map/ppermute | solution.py:17
  175.6 4.3 collective-permute-start.11
  180.3 0.5 collective-permute-done.11
  187.6 0.8 convert_element_type.62
  188.4 244.0 %all-reduce.3.cloned.1.call-done = (f32[64,1728]{1,0:T(8,128)}, f32[64,1728]{1,0:T(8,128)}) async-done(((f32[64,1728]{1,0:T(8,128)}, f32[64,1728]{1,0:T(8,128)}), (f32[64,1728]{1,0:T(8,128)}, f32[64,1728]{1,0:T(8,128)})) %all-reduce.3.cloned.1.call-update) | async-done | bytes 884752 | tf_op jit(solution)/shard_map/psum | solution.py:110
  432.5 1.4 constant_dynamic-slice_fusion.1
  433.9 1.4 constant_dynamic-slice_fusion
  (199 shorter events, 21.6 us)
Async XLA Ops:
  7.2 425.3 %all-reduce.3.cloned.1.call-start = ((), (), s32[]{:S(2)}) async-start(), calls=%async_computation | async-start | bytes 1835008 | tf_op jit(solution)/shard_map/psum | solution.py:110
  11.0 14.6 %copy-start.5 = (bf16[4,8,1024]{2,1,0:T(8,128)(2,1)S(1)}, bf16[4,8,1024]{2,1,0:T(8,128)(2,1)}, u32[]{:S(2)}) copy-start(bf16[4,8,1024]{2,1,0:T(8,128)(2,1)} %param.8) | copy-start | bytes 196612
  11.3 14.8 %copy-start.36 = (bf16[4,1728]{1,0:T(4,128)(2,1)S(1)}, bf16[4,1728]{1,0:T(4,128)(2,1)}, u32[]{:S(2)}) copy-start(bf16[4,1728]{1,0:T(4,128)(2,1)} %param.11) | copy-start | bytes 41476
  11.3 68.8 %collective-permute-start.1 = (bf16[1,8,16,192]{3,2,1,0:T(8,128)(2,1)S(1)}, bf16[1,8,16,192]{3,2,1,0:T(8,128)(2,1)S(1)}, u32[]{:S(2)}, u32[]{:S(2)}) collective-permute-start(bf16[1,8,16,192]{3,2,1,0:T(8,128)(2,1)S(1)} %get-tuple-element.68), channel_id=1, source_target_pairs={{32,0},{64,32},{96,64},{128,96},{160,128},{192,160},{224,192},{256... | collective-permute-start | bytes 147464 | tf_op jit(solution)/shard_map/ppermute | solution.py:17
  23.7 56.4 %collective-permute-start = (bf16[1,8,16,192]{3,2,1,0:T(8,128)(2,1)S(1)}, bf16[1,8,16,192]{3,2,1,0:T(8,128)(2,1)S(1)}, u32[]{:S(2)}, u32[]{:S(2)}) collective-permute-start(bf16[1,8,16,192]{3,2,1,0:T(8,128)(2,1)S(1)} %get-tuple-element.67), channel_id=1, source_target_pairs={{0,32},{32,64},{64,96},{96,128},{128,160},{160,192},{192,224},{224... | collective-permute-start | bytes 147464 | tf_op jit(solution)/shard_map/ppermute | solution.py:14
  53.6 1.2 copy-start.37
  53.6 25.3 %copy-start.6 = (bf16[4,8,1024]{2,1,0:T(8,128)(2,1)S(1)}, bf16[4,8,1024]{2,1,0:T(8,128)(2,1)}, u32[]{:S(2)}) copy-start(bf16[4,8,1024]{2,1,0:T(8,128)(2,1)} %param.7) | copy-start | bytes 196612
  53.8 25.3 %copy-start.7 = (bf16[4,8,1024]{2,1,0:T(8,128)(2,1)S(1)}, bf16[4,8,1024]{2,1,0:T(8,128)(2,1)}, u32[]{:S(2)}) copy-start(bf16[4,8,1024]{2,1,0:T(8,128)(2,1)} %param.6) | copy-start | bytes 196612
  80.2 7.9 %collective-permute-start.3 = (bf16[6,1,16,192]{3,2,1,0:T(8,128)(2,1)S(1)}, bf16[6,1,16,192]{3,2,1,0:T(8,128)(2,1)S(1)}, u32[]{:S(2)}, u32[]{:S(2)}) collective-permute-start(bf16[6,1,16,192]{3,2,1,0:T(8,128)(2,1)S(1)} %get-tuple-element.48), channel_id=1, source_target_pairs={{4,0},{8,4},{12,8},{16,12},{20,16},{24,20},{28,24},{0,28},{5,1},{9... | collective-permute-start | bytes 110600 | tf_op jit(solution)/shard_map/ppermute | solution.py:17
  85.3 6.3 %collective-permute-start.2 = (bf16[6,1,16,192]{3,2,1,0:T(8,128)(2,1)S(1)}, bf16[6,1,16,192]{3,2,1,0:T(8,128)(2,1)S(1)}, u32[]{:S(2)}, u32[]{:S(2)}) collective-permute-start(bf16[6,1,16,192]{3,2,1,0:T(8,128)(2,1)S(1)} %get-tuple-element.47), channel_id=1, source_target_pairs={{0,4},{4,8},{8,12},{12,16},{16,20},{20,24},{24,28},{28,0},{1,5},{5... | collective-permute-start | bytes 110600 | tf_op jit(solution)/shard_map/ppermute | solution.py:14
  91.9 23.3 %collective-permute-start.4 = (bf16[6,10,1,192]{3,2,1,0:T(2,128)(2,1)S(1)}, bf16[6,10,1,192]{3,2,1,0:T(2,128)(2,1)S(1)}, u32[]{:S(2)}, u32[]{:S(2)}) collective-permute-start(bf16[6,10,1,192]{3,2,1,0:T(2,128)(2,1)S(1)} %get-tuple-element.43), channel_id=1, source_target_pairs={{1,0},{2,1},{3,2},{0,3},{5,4},{6,5},{7,6},{4,7},{9,8},{10,9},{11,1... | collective-permute-start | bytes 69128 | tf_op jit(solution)/shard_map/ppermute | solution.py:17
  110.1 5.5 %collective-permute-start.5 = (bf16[6,10,1,192]{3,2,1,0:T(2,128)(2,1)S(1)}, bf16[6,10,1,192]{3,2,1,0:T(2,128)(2,1)S(1)}, u32[]{:S(2)}, u32[]{:S(2)}) collective-permute-start(bf16[6,10,1,192]{3,2,1,0:T(2,128)(2,1)S(1)} %get-tuple-element.44), channel_id=1, source_target_pairs={{0,1},{1,2},{2,3},{3,0},{4,5},{5,6},{6,7},{7,4},{8,9},{9,10},{10,1... | collective-permute-start | bytes 69128 | tf_op jit(solution)/shard_map/ppermute | solution.py:14
  143.0 1.0 copy-start.3
  146.2 0.9 copy-start.8
  147.3 8.4 %copy-start.2 = (bf16[4,8,16,64]{3,2,1,0:T(8,128)(2,1)S(1)}, bf16[4,8,16,64]{3,2,1,0:T(8,128)(2,1)}, u32[]{:S(2)}) copy-start(bf16[4,8,16,64]{3,2,1,0:T(8,128)(2,1)} %get-tuple-element.12) | copy-start | bytes 196612
  148.1 14.2 %collective-permute-start.7 = (bf16[1,8,16,64]{3,2,1,0:T(8,128)(2,1)}, bf16[1,8,16,64]{3,2,1,0:T(8,128)(2,1)S(1)}, u32[]{:S(2)}, u32[]{:S(2)}) collective-permute-start(bf16[1,8,16,64]{3,2,1,0:T(8,128)(2,1)} %bitcast.33), channel_id=1, source_target_pairs={{32,0},{64,32},{96,64},{128,96},{160,128},{192,160},{224,192},{256... | collective-permute-start | bytes 49160 | tf_op jit(solution)/shard_map/ppermute | solution.py:17
  151.7 10.6 %collective-permute-start.6 = (bf16[1,8,16,64]{3,2,1,0:T(8,128)(2,1)}, bf16[1,8,16,64]{3,2,1,0:T(8,128)(2,1)S(1)}, u32[]{:S(2)}, u32[]{:S(2)}) collective-permute-start(bf16[1,8,16,64]{3,2,1,0:T(8,128)(2,1)} %bitcast.31), channel_id=1, source_target_pairs={{0,32},{32,64},{64,96},{96,128},{128,160},{160,192},{192,224},{224... | collective-permute-start | bytes 49160 | tf_op jit(solution)/shard_map/ppermute | solution.py:14
  154.4 1.9 copy-start.1
  155.7 1.0 copy-start
  157.5 1.0 copy-start.4
  159.5 1.1 copy-start.9
  159.5 1.1 copy-start.10
  159.5 1.1 copy-start.11
  159.5 1.1 copy-start.12
  159.6 1.1 copy-start.13
  159.6 1.1 copy-start.14
  159.6 1.1 copy-start.15
  159.6 1.1 copy-start.16
  159.6 1.1 copy-start.17
  159.6 1.1 copy-start.18
  159.6 1.1 copy-start.19
  159.6 1.1 copy-start.20
  159.6 1.1 copy-start.21
  159.6 1.1 copy-start.22
  159.7 1.1 copy-start.23
  159.7 1.1 copy-start.24
  159.7 1.1 copy-start.25
  159.7 1.1 copy-start.26
  159.7 1.1 copy-start.27
  159.7 1.1 copy-start.28
  159.7 1.1 copy-start.29
  159.7 1.1 copy-start.30
  159.7 1.1 copy-start.31
  159.7 1.1 copy-start.32
  159.8 1.1 copy-start.33
  159.8 1.1 copy-start.34
  159.8 1.1 copy-start.35
  162.4 5.5 %collective-permute-start.9 = (bf16[6,1,16,64]{3,2,1,0:T(8,128)(2,1)S(1)}, bf16[6,1,16,64]{3,2,1,0:T(8,128)(2,1)S(1)}, u32[]{:S(2)}, u32[]{:S(2)}) collective-permute-start(bf16[6,1,16,64]{3,2,1,0:T(8,128)(2,1)S(1)} %get-tuple-element.100), channel_id=1, source_target_pairs={{4,0},{8,4},{12,8},{16,12},{20,16},{24,20},{28,24},{0,28},{5,1},{9... | collective-permute-start | bytes 36872 | tf_op jit(solution)/shard_map/ppermute | solution.py:17
  164.5 5.8 %collective-permute-start.8 = (bf16[6,1,16,64]{3,2,1,0:T(8,128)(2,1)S(1)}, bf16[6,1,16,64]{3,2,1,0:T(8,128)(2,1)S(1)}, u32[]{:S(2)}, u32[]{:S(2)}) collective-permute-start(bf16[6,1,16,64]{3,2,1,0:T(8,128)(2,1)S(1)} %get-tuple-element.99), channel_id=1, source_target_pairs={{0,4},{4,8},{8,12},{12,16},{16,20},{20,24},{24,28},{28,0},{1,5},{5... | collective-permute-start | bytes 36872 | tf_op jit(solution)/shard_map/ppermute | solution.py:14
  170.3 10.0 %collective-permute-start.10 = (bf16[6,10,1,64]{3,2,1,0:T(2,128)(2,1)S(1)}, bf16[6,10,1,64]{3,2,1,0:T(2,128)(2,1)S(1)}, u32[]{:S(2)}, u32[]{:S(2)}) collective-permute-start(bf16[6,10,1,64]{3,2,1,0:T(2,128)(2,1)S(1)} %get-tuple-element.89), channel_id=1, source_target_pairs={{1,0},{2,1},{3,2},{0,3},{5,4},{6,5},{7,6},{4,7},{9,8},{10,9},{11,1... | collective-permute-start | bytes 23048 | tf_op jit(solution)/shard_map/ppermute | solution.py:17
  175.6 5.2 %collective-permute-start.11 = (bf16[6,10,1,64]{3,2,1,0:T(2,128)(2,1)S(1)}, bf16[6,10,1,64]{3,2,1,0:T(2,128)(2,1)S(1)}, u32[]{:S(2)}, u32[]{:S(2)}) collective-permute-start(bf16[6,10,1,64]{3,2,1,0:T(2,128)(2,1)S(1)} %get-tuple-element.90), channel_id=1, source_target_pairs={{0,1},{1,2},{2,3},{3,0},{4,5},{5,6},{6,7},{7,4},{8,9},{9,10},{10,1... | collective-permute-start | bytes 23048 | tf_op jit(solution)/shard_map/ppermute | solution.py:14
Sparse Core Ops, SparseCore 0:
  162.4 269.9 all-reduce.2
where the time goes:
time: 443 us; the launch traced here: 442 us
  waiting for transfers between devices  251 us (57%)
  starting transfers between devices  64.1 us (14%)
  blocking collectives  51.5 us (12%)
  matrix products  40.7 us (9%)
  between operations  15 us (3%)
  local copies, waits for them, and re-layouts  13.2 us (3%)
  other arithmetic  6.58 us (1%)
    psum x1, waiting for transfers between devices, body(): lax.psum((grads_one, grads_two), ('gx', 'gy', 'gz'))  244 us
    ppermute x6, starting transfers between devices, padded_2(): lax.ppermute(lax.slice_in_dim(block, 0, width, axis=dim), axis, backward)  46.1 us
    all_gather x1, blocking collectives, body(): lax.all_gather(conv2_weight, 'gx', axis=0, tiled=True)  27.4 us
    dot_general x54, matrix products, weight_grad(): lax.dot_general(left_flat, ahead, (((0,), (0,)), ((), ())), preferred_ele...  26.9 us
    all_gather x1, blocking collectives, body(): lax.all_gather(conv1_weight, 'gx', axis=0, tiled=True)  24.1 us
    ppermute x6, starting transfers between devices, padded_2(): lax.ppermute(lax.slice_in_dim(block, block.shape[dim] - width, None, axis...  18.1 us
    dot_general x54, matrix products, transpose_conv(): lax.dot_general(behind, block, (((1,), (0,)), ((), ())), preferred_elemen...  13.8 us
  transfers between devices with their start and end apart: 13, of which 5 were waited for; matrix products, arithmetic and copies ran while one was open for 5% of the time, Pallas kernels for 0%

commit v1 on v0

--- a/solution.py
+++ b/solution.py
@@ -3,6 +3,11 @@
 import jax.numpy as jnp
 from jax import lax
 from jax.sharding import PartitionSpec as P
+
+
+def exchange_gather(x, name, dim):
+    stack = jnp.stack([x] * lax.axis_size(name))
+    return jnp.concatenate(lax.all_to_all(stack, name, 0, 0), axis=dim)
 
 
 def padded_2(block, sides, width):
@@ -68,7 +73,7 @@
     inner = (size_x, size_y, size_z)
     four_shape = (size_x, size_y, size_z, chans)
     weight_one, weight_two = (
-        lax.all_gather(conv1_weight, "gx", axis=0, tiled=True),
+        exchange_gather(conv1_weight, "gx", 0),
         lax.all_gather(conv2_weight, "gx", axis=0, tiled=True),
     )
     pool_four = pool_grad.reshape(size_x // 2, size_y // 2, size_z // 2, chans).astype(jnp.float32)

time: 443 us -> 421 us (0.950)
  blocking collectives: 51.5 us -> 27.7 us
    all_gather x1 -> x0, blocking collectives: 24.1 us -> none  [body(): lax.all_gather(conv1_weight, 'gx', axis=0, tiled=True)]
    ppermute x6, starting transfers between devices: 46.1 us -> 38.7 us  [padded_2(): lax.ppermute(lax.slice_in_dim(block, 0, width, axis=dim), axis, backward)]
    all_to_all x0 -> x1, starting transfers between devices: none -> 4.94 us  [exchange_gather(): return jnp.concatenate(lax.all_to_all(stack, name, 0, 0), axis=dim)]
  transfers between devices with their start and end apart: 13 -> 14, of which waited for: 5 -> 4; matrix products, arithmetic and copies ran while one was open for 5% -> 14% of each run, Pallas kernels for 0% -> 0%
where the time goes in v1:
time: 421 us; the launch traced here: 420 us
  waiting for transfers between devices  248 us (59%)
  starting transfers between devices  62.9 us (15%)
  matrix products  41.5 us (10%)
  blocking collectives  27.7 us (7%)
  local copies, waits for them, and re-layouts  17.2 us (4%)
  between operations  15 us (4%)
  other arithmetic  7.28 us (2%)
    psum x1, waiting for transfers between devices, body(): lax.psum((grads_one, grads_two), ('gx', 'gy', 'gz'))  243 us
    ppermute x6, starting transfers between devices, padded_2(): lax.ppermute(lax.slice_in_dim(block, 0, width, axis=dim), axis, backward)  38.7 us
    dot_general x54, matrix products, weight_grad(): lax.dot_general(left_flat, ahead, (((0,), (0,)), ((), ())), preferred_ele...  27.8 us
    all_gather x1, blocking collectives, body(): lax.all_gather(conv2_weight, 'gx', axis=0, tiled=True)  27.7 us
    ppermute x6, starting transfers between devices, padded_2(): lax.ppermute(lax.slice_in_dim(block, block.shape[dim] - width, None, axis...  19.2 us
    dot_general x54, matrix products, transpose_conv(): lax.dot_general(behind, block, (((1,), (0,)), ((), ())), preferred_elemen...  13.8 us
  transfers between devices with their start and end apart: 14, of which 4 were waited for; matrix products, arithmetic and copies ran while one was open for 14% of the time, Pallas kernels for 0%

profile of v1, /device:TPU:1, one launch (start us, length us, event | category | flops | bytes accessed | tf_op | source)
XLA Modules:
  0.0 419.7 jit_solution(6956273285536803984)
XLA Ops:
  7.2 1.0 reshape.410
  8.9 1.0 reshape.327
  9.9 1.0 reshape.326
  11.3 12.4 %collective-permute-start.1 = (bf16[1,8,16,192]{3,2,1,0:T(8,128)(2,1)S(1)}, bf16[1,8,16,192]{3,2,1,0:T(8,128)(2,1)S(1)}, u32[]{:S(2)}, u32[]{:S(2)}) collective-permute-start(bf16[1,8,16,192]{3,2,1,0:T(8,128)(2,1)S(1)} %get-tuple-element.68), channel_id=1, source_target_pairs={{32,0},{64,32},{96,64},{128,96},{160,128},{192,160},{224,192},{256... | collective-permute-start | bytes 147464 | tf_op jit(solution)/shard_map/ppermute | solution.py:22
  23.7 1.9 collective-permute-start
  25.6 0.8 stack.2
  26.4 4.9 %all-to-all-start = ((bf16[16,4,1728]{2,1,0:T(4,128)(2,1)}), bf16[16,4,1728]{2,1,0:T(4,128)(2,1)S(1)}, u32[]{:S(2)}, u32[]{:S(2)}) async-start(bf16[16,4,1728]{2,1,0:T(4,128)(2,1)} %stack.2), calls=%async_computation | async-start | bytes 458752 | tf_op jit(solution)/shard_map/all_to_all | solution.py:10
  31.5 27.7 %all-gather = bf16[16,4,1728]{2,1,0:T(4,128)(2,1)S(1)} all-gather(bf16[1,4,1728]{2,1,0:T(4,128)(2,1)S(1)} %bitcast.416), channel_id=1, replica_groups=mesh['gx'=16,'gy'=8,'gz'=4] {'gx'}, dimensions={0}, use_global_device_ids=true | all-gather | bytes 235008 | tf_op jit(solution)/shard_map/all_gather | solution.py:77
  59.6 0.9 fusion.86
  61.5 0.8 copy.24
  62.4 5.1 %collective-permute-start.3 = (bf16[6,1,16,192]{3,2,1,0:T(8,128)(2,1)S(1)}, bf16[6,1,16,192]{3,2,1,0:T(8,128)(2,1)S(1)}, u32[]{:S(2)}, u32[]{:S(2)}) collective-permute-start(bf16[6,1,16,192]{3,2,1,0:T(8,128)(2,1)S(1)} %get-tuple-element.48), channel_id=1, source_target_pairs={{4,0},{8,4},{12,8},{16,12},{20,16},{24,20},{28,24},{0,28},{5,1},{9... | collective-permute-start | bytes 110600 | tf_op jit(solution)/shard_map/ppermute | solution.py:22
  67.5 1.9 collective-permute-start.2
  69.4 0.9 pad_maximum_fusion.10
  70.3 3.2 collective-permute-done.2
  73.8 12.1 %collective-permute-start.4 = (bf16[6,10,1,192]{3,2,1,0:T(2,128)(2,1)S(1)}, bf16[6,10,1,192]{3,2,1,0:T(2,128)(2,1)S(1)}, u32[]{:S(2)}, u32[]{:S(2)}) collective-permute-start(bf16[6,10,1,192]{3,2,1,0:T(2,128)(2,1)S(1)} %get-tuple-element.43), channel_id=1, source_target_pairs={{1,0},{2,1},{3,2},{0,3},{5,4},{6,5},{7,6},{4,7},{9,8},{10,9},{11,1... | collective-permute-start | bytes 69128 | tf_op jit(solution)/shard_map/ppermute | solution.py:22
  85.9 4.3 %collective-permute-start.5 = (bf16[6,10,1,192]{3,2,1,0:T(2,128)(2,1)S(1)}, bf16[6,10,1,192]{3,2,1,0:T(2,128)(2,1)S(1)}, u32[]{:S(2)}, u32[]{:S(2)}) collective-permute-start(bf16[6,10,1,192]{3,2,1,0:T(2,128)(2,1)S(1)} %get-tuple-element.44), channel_id=1, source_target_pairs={{0,1},{1,2},{2,3},{3,0},{4,5},{5,6},{6,7},{7,4},{8,9},{9,10},{10,1... | collective-permute-start | bytes 69128 | tf_op jit(solution)/shard_map/ppermute | solution.py:19
  91.9 0.8 convolution_bitcast_fusion.26
  92.8 0.8 convolution_bitcast_fusion.25
  93.6 0.8 convolution_bitcast_fusion.24
  94.4 0.8 convolution_bitcast_fusion.23
  95.2 0.8 convolution_bitcast_fusion.22
  96.0 0.8 convolution_bitcast_fusion.21
  96.8 0.8 convolution_bitcast_fusion.20
  97.6 0.8 convolution_bitcast_fusion.19
  98.5 0.8 convolution_bitcast_fusion.18
  99.3 0.8 convolution_bitcast_fusion.17
  100.1 0.8 convolution_bitcast_fusion.16
  100.9 0.8 convolution_bitcast_fusion.15
  101.7 0.8 convolution_bitcast_fusion.14
  102.5 0.8 convolution_bitcast_fusion.13
  103.3 0.8 convolution_bitcast_fusion.12
  104.2 0.8 convolution_bitcast_fusion.11
  105.0 0.8 convolution_bitcast_fusion.10
  105.8 0.8 convolution_bitcast_fusion.9
  106.6 0.8 convolution_bitcast_fusion.8
  107.4 0.8 convolution_bitcast_fusion.7
  108.2 0.8 convolution_bitcast_fusion.6
  109.1 0.8 convolution_bitcast_fusion.5
  109.9 0.8 convolution_bitcast_fusion.4
  110.7 0.8 convolution_bitcast_fusion.3
  111.5 0.8 convolution_bitcast_fusion.2
  112.3 0.8 convolution_bitcast_fusion.1
  113.1 0.8 convolution_bitcast_fusion
  113.9 1.4 pad_maximum_fusion
  116.3 1.3 fusion.103
  123.3 0.7 copy.28
  124.0 1.9 collective-permute-start.7
  126.6 3.5 collective-permute-start.6
  130.5 0.8 fusion.114
  131.4 1.1 fusion.116
  136.5 0.8 broadcast_multiply_fusion.1
  137.8 0.8 broadcast_multiply_fusion
  138.8 1.9 collective-permute-start.9
  140.8 3.4 collective-permute-start.8
  144.8 1.7 collective-permute-done.8
  146.6 5.3 %collective-permute-start.10 = (bf16[6,10,1,64]{3,2,1,0:T(2,128)(2,1)S(1)}, bf16[6,10,1,64]{3,2,1,0:T(2,128)(2,1)S(1)}, u32[]{:S(2)}, u32[]{:S(2)}) collective-permute-start(bf16[6,10,1,64]{3,2,1,0:T(2,128)(2,1)S(1)} %get-tuple-element.89), channel_id=1, source_target_pairs={{1,0},{2,1},{3,2},{0,3},{5,4},{6,5},{7,6},{4,7},{9,8},{10,9},{11,1... | collective-permute-start | bytes 23048 | tf_op jit(solution)/shard_map/ppermute | solution.py:22
  151.9 4.3 %collective-permute-start.11 = (bf16[6,10,1,64]{3,2,1,0:T(2,128)(2,1)S(1)}, bf16[6,10,1,64]{3,2,1,0:T(2,128)(2,1)S(1)}, u32[]{:S(2)}, u32[]{:S(2)}) collective-permute-start(bf16[6,10,1,64]{3,2,1,0:T(2,128)(2,1)S(1)} %get-tuple-element.90), channel_id=1, source_target_pairs={{0,1},{1,2},{2,3},{3,0},{4,5},{5,6},{6,7},{7,4},{8,9},{9,10},{10,1... | collective-permute-start | bytes 23048 | tf_op jit(solution)/shard_map/ppermute | solution.py:19
  156.2 0.8 fusion.110
  157.0 0.8 fusion.109
  158.3 0.9 fusion.108
  166.6 0.8 convert_element_type.62
  167.4 242.7 %all-reduce.3.cloned.1.call-done = (f32[64,1728]{1,0:T(8,128)}, f32[64,1728]{1,0:T(8,128)}) async-done(((f32[64,1728]{1,0:T(8,128)}, f32[64,1728]{1,0:T(8,128)}), (f32[64,1728]{1,0:T(8,128)}, f32[64,1728]{1,0:T(8,128)})) %all-reduce.3.cloned.1.call-update) | async-done | bytes 884752 | tf_op jit(solution)/shard_map/psum | solution.py:115
  410.0 1.4 constant_dynamic-slice_fusion.1
  411.5 1.4 constant_dynamic-slice_fusion
  (219 shorter events, 25.2 us)
Async XLA Ops:
  11.0 14.7 %copy-start.45 = (bf16[4,1728]{1,0:T(4,128)(2,1)S(1)}, bf16[4,1728]{1,0:T(4,128)(2,1)}, u32[]{:S(2)}) copy-start(bf16[4,1728]{1,0:T(4,128)(2,1)} %param.10) | copy-start | bytes 41476
  11.1 20.3 %copy-start.13 = (bf16[4,8,1024]{2,1,0:T(8,128)(2,1)S(1)}, bf16[4,8,1024]{2,1,0:T(8,128)(2,1)}, u32[]{:S(2)}) copy-start(bf16[4,8,1024]{2,1,0:T(8,128)(2,1)} %param.8) | copy-start | bytes 196612
  11.1 20.4 %copy-start.46 = (bf16[4,1728]{1,0:T(4,128)(2,1)S(1)}, bf16[4,1728]{1,0:T(4,128)(2,1)}, u32[]{:S(2)}) copy-start(bf16[4,1728]{1,0:T(4,128)(2,1)} %param.11) | copy-start | bytes 41476
  11.3 51.0 %collective-permute-start.1 = (bf16[1,8,16,192]{3,2,1,0:T(8,128)(2,1)S(1)}, bf16[1,8,16,192]{3,2,1,0:T(8,128)(2,1)S(1)}, u32[]{:S(2)}, u32[]{:S(2)}) collective-permute-start(bf16[1,8,16,192]{3,2,1,0:T(8,128)(2,1)S(1)} %get-tuple-element.68), channel_id=1, source_target_pairs={{32,0},{64,32},{96,64},{128,96},{160,128},{192,160},{224,192},{256... | collective-permute-start | bytes 147464 | tf_op jit(solution)/shard_map/ppermute | solution.py:22
  23.7 38.6 %collective-permute-start = (bf16[1,8,16,192]{3,2,1,0:T(8,128)(2,1)S(1)}, bf16[1,8,16,192]{3,2,1,0:T(8,128)(2,1)S(1)}, u32[]{:S(2)}, u32[]{:S(2)}) collective-permute-start(bf16[1,8,16,192]{3,2,1,0:T(8,128)(2,1)S(1)} %get-tuple-element.67), channel_id=1, source_target_pairs={{0,32},{32,64},{64,96},{96,128},{128,160},{160,192},{192,224},{224... | collective-permute-start | bytes 147464 | tf_op jit(solution)/shard_map/ppermute | solution.py:19
  26.4 132.7 %all-to-all-start = ((bf16[16,4,1728]{2,1,0:T(4,128)(2,1)}), bf16[16,4,1728]{2,1,0:T(4,128)(2,1)S(1)}, u32[]{:S(2)}, u32[]{:S(2)}) async-start(bf16[16,4,1728]{2,1,0:T(4,128)(2,1)} %stack.2), calls=%async_computation | async-start | bytes 458752 | tf_op jit(solution)/shard_map/all_to_all | solution.py:10
  31.3 378.7 %all-reduce.3.cloned.1.call-start = ((), (), s32[]{:S(2)}) async-start(), calls=%async_computation.1 | async-start | bytes 1835008 | tf_op jit(solution)/shard_map/psum | solution.py:115
  59.6 1.3 copy-start.14
  60.5 0.8 copy-start.15
  62.4 7.9 %collective-permute-start.3 = (bf16[6,1,16,192]{3,2,1,0:T(8,128)(2,1)S(1)}, bf16[6,1,16,192]{3,2,1,0:T(8,128)(2,1)S(1)}, u32[]{:S(2)}, u32[]{:S(2)}) collective-permute-start(bf16[6,1,16,192]{3,2,1,0:T(8,128)(2,1)S(1)} %get-tuple-element.48), channel_id=1, source_target_pairs={{4,0},{8,4},{12,8},{16,12},{20,16},{24,20},{28,24},{0,28},{5,1},{9... | collective-permute-start | bytes 110600 | tf_op jit(solution)/shard_map/ppermute | solution.py:22
  67.5 6.0 %collective-permute-start.2 = (bf16[6,1,16,192]{3,2,1,0:T(8,128)(2,1)S(1)}, bf16[6,1,16,192]{3,2,1,0:T(8,128)(2,1)S(1)}, u32[]{:S(2)}, u32[]{:S(2)}) collective-permute-start(bf16[6,1,16,192]{3,2,1,0:T(8,128)(2,1)S(1)} %get-tuple-element.47), channel_id=1, source_target_pairs={{0,4},{4,8},{8,12},{12,16},{16,20},{20,24},{24,28},{28,0},{1,5},{5... | collective-permute-start | bytes 110600 | tf_op jit(solution)/shard_map/ppermute | solution.py:19
  73.8 17.2 %collective-permute-start.4 = (bf16[6,10,1,192]{3,2,1,0:T(2,128)(2,1)S(1)}, bf16[6,10,1,192]{3,2,1,0:T(2,128)(2,1)S(1)}, u32[]{:S(2)}, u32[]{:S(2)}) collective-permute-start(bf16[6,10,1,192]{3,2,1,0:T(2,128)(2,1)S(1)} %get-tuple-element.43), channel_id=1, source_target_pairs={{1,0},{2,1},{3,2},{0,3},{5,4},{6,5},{7,6},{4,7},{9,8},{10,9},{11,1... | collective-permute-start | bytes 69128 | tf_op jit(solution)/shard_map/ppermute | solution.py:22
  85.9 5.5 %collective-permute-start.5 = (bf16[6,10,1,192]{3,2,1,0:T(2,128)(2,1)S(1)}, bf16[6,10,1,192]{3,2,1,0:T(2,128)(2,1)S(1)}, u32[]{:S(2)}, u32[]{:S(2)}) collective-permute-start(bf16[6,10,1,192]{3,2,1,0:T(2,128)(2,1)S(1)} %get-tuple-element.44), channel_id=1, source_target_pairs={{0,1},{1,2},{2,3},{3,0},{4,5},{5,6},{6,7},{7,4},{8,9},{9,10},{10,1... | collective-permute-start | bytes 69128 | tf_op jit(solution)/shard_map/ppermute | solution.py:19
  119.0 1.0 copy-start.11
  122.1 0.9 copy-start.16
  123.2 9.2 %copy-start.2 = (bf16[4,8,16,64]{3,2,1,0:T(8,128)(2,1)S(1)}, bf16[4,8,16,64]{3,2,1,0:T(8,128)(2,1)}, u32[]{:S(2)}) copy-start(bf16[4,8,16,64]{3,2,1,0:T(8,128)(2,1)} %get-tuple-element.12) | copy-start | bytes 196612
  124.0 14.8 %collective-permute-start.7 = (bf16[1,8,16,64]{3,2,1,0:T(8,128)(2,1)}, bf16[1,8,16,64]{3,2,1,0:T(8,128)(2,1)S(1)}, u32[]{:S(2)}, u32[]{:S(2)}) collective-permute-start(bf16[1,8,16,64]{3,2,1,0:T(8,128)(2,1)} %bitcast.33), channel_id=1, source_target_pairs={{32,0},{64,32},{96,64},{128,96},{160,128},{192,160},{224,192},{256... | collective-permute-start | bytes 49160 | tf_op jit(solution)/shard_map/ppermute | solution.py:22
  126.6 12.2 %collective-permute-start.6 = (bf16[1,8,16,64]{3,2,1,0:T(8,128)(2,1)}, bf16[1,8,16,64]{3,2,1,0:T(8,128)(2,1)S(1)}, u32[]{:S(2)}, u32[]{:S(2)}) collective-permute-start(bf16[1,8,16,64]{3,2,1,0:T(8,128)(2,1)} %bitcast.31), channel_id=1, source_target_pairs={{0,32},{32,64},{64,96},{96,128},{128,160},{160,192},{192,224},{224... | collective-permute-start | bytes 49160 | tf_op jit(solution)/shard_map/ppermute | solution.py:19
  130.5 2.5 copy-start.1
  132.5 1.0 copy-start
  134.2 1.0 copy-start.12
  135.0 1.0 copy-start.17
  136.2 1.1 copy-start.18
  136.2 1.1 copy-start.19
  136.3 1.1 copy-start.20
  136.3 1.1 copy-start.21
  136.3 1.1 copy-start.22
  136.3 1.1 copy-start.23
  136.3 1.1 copy-start.24
  136.3 1.1 copy-start.25
  136.3 1.1 copy-start.26
  136.3 1.1 copy-start.27
  136.3 1.1 copy-start.28
  136.3 1.1 copy-start.29
  136.4 1.1 copy-start.30
  136.4 1.1 copy-start.31
  136.4 1.1 copy-start.32
  136.4 1.1 copy-start.33
  136.4 1.1 copy-start.34
  136.4 1.1 copy-start.35
  136.4 1.1 copy-start.36
  136.4 1.1 copy-start.37
  136.4 1.1 copy-start.38
  136.4 1.1 copy-start.39
  136.5 1.1 copy-start.40
  136.5 1.1 copy-start.41
  136.5 1.1 copy-start.42
  136.5 1.1 copy-start.43
  136.5 1.1 copy-start.44
  138.8 6.0 %collective-permute-start.9 = (bf16[6,1,16,64]{3,2,1,0:T(8,128)(2,1)S(1)}, bf16[6,1,16,64]{3,2,1,0:T(8,128)(2,1)S(1)}, u32[]{:S(2)}, u32[]{:S(2)}) collective-permute-start(bf16[6,1,16,64]{3,2,1,0:T(8,128)(2,1)S(1)} %get-tuple-element.100), channel_id=1, source_target_pairs={{4,0},{8,4},{12,8},{16,12},{20,16},{24,20},{28,24},{0,28},{5,1},{9... | collective-permute-start | bytes 36872 | tf_op jit(solution)/shard_map/ppermute | solution.py:22
  140.8 5.8 %collective-permute-start.8 = (bf16[6,1,16,64]{3,2,1,0:T(8,128)(2,1)S(1)}, bf16[6,1,16,64]{3,2,1,0:T(8,128)(2,1)S(1)}, u32[]{:S(2)}, u32[]{:S(2)}) collective-permute-start(bf16[6,1,16,64]{3,2,1,0:T(8,128)(2,1)S(1)} %get-tuple-element.99), channel_id=1, source_target_pairs={{0,4},{4,8},{8,12},{12,16},{16,20},{20,24},{24,28},{28,0},{1,5},{5... | collective-permute-start | bytes 36872 | tf_op jit(solution)/shard_map/ppermute | solution.py:19
  146.6 11.2 %collective-permute-start.10 = (bf16[6,10,1,64]{3,2,1,0:T(2,128)(2,1)S(1)}, bf16[6,10,1,64]{3,2,1,0:T(2,128)(2,1)S(1)}, u32[]{:S(2)}, u32[]{:S(2)}) collective-permute-start(bf16[6,10,1,64]{3,2,1,0:T(2,128)(2,1)S(1)} %get-tuple-element.89), channel_id=1, source_target_pairs={{1,0},{2,1},{3,2},{0,3},{5,4},{6,5},{7,6},{4,7},{9,8},{10,9},{11,1... | collective-permute-start | bytes 23048 | tf_op jit(solution)/shard_map/ppermute | solution.py:22
  151.9 6.0 %collective-permute-start.11 = (bf16[6,10,1,64]{3,2,1,0:T(2,128)(2,1)S(1)}, bf16[6,10,1,64]{3,2,1,0:T(2,128)(2,1)S(1)}, u32[]{:S(2)}, u32[]{:S(2)}) collective-permute-start(bf16[6,10,1,64]{3,2,1,0:T(2,128)(2,1)S(1)} %get-tuple-element.90), channel_id=1, source_target_pairs={{0,1},{1,2},{2,3},{3,0},{4,5},{5,6},{6,7},{7,4},{8,9},{9,10},{10,1... | collective-permute-start | bytes 23048 | tf_op jit(solution)/shard_map/ppermute | solution.py:19
  159.1 0.9 copy-start.10
  160.1 1.0 copy-start.5
  160.8 0.9 copy-start.8
  161.3 1.2 copy-start.7
  162.0 1.0 copy-start.9
  163.0 0.9 copy-start.6
  163.4 1.2 copy-start.4
  165.1 0.9 copy-start.3
Sparse Core Ops, SparseCore 0:
  138.9 271.0 all-reduce.2
